TPU v7x, 256 devices: a whole 4x4x8 slice. The times are simulated.
256 devices in a mesh: pts: 64 (over y, z, core), grp: 4 (over x).
Axes of the slice: x: 4, y: 4, z: 8, core: 2. Of those that a mesh axis runs over, the one named last changes fastest.
Arguments:
- spectrum: float32 [4, 1152, 8192], P('grp', None, 'pts'), may hold values from 0.05 to 1
- coarse_spectra: float32 [4, 1152, 1024], P('grp', None, 'pts'), may hold values from 0.05 to 1
- wind_east: float32 [4, 8192], P('grp', 'pts'), may hold values from -6 to 6
- wind_north: float32 [4, 8192], P('grp', 'pts'), may hold values from -6 to 6
- refraction: float32 [4, 8192], P('grp', 'pts'), may hold values from -0.8 to 0.8
- freq_kernel: float32 [32, 32], replicated, may hold values from -1 to 1
- sea_mask: int32 [4, 8192], P('grp'), may hold values from 0 to 1, as said below
- upwind_lists: int32 [4, 4, 8192], P('grp'), may hold values from 0 to 9215, as said below
- boundary_list: int32 [4, 1024], P('grp', 'pts'), may hold values from 0 to 4095, as said below
Outputs:
- spectrum_out: float32 [4, 1152, 8192], P('grp', None, 'pts')
Inputs may be any that keep to these rules, and one draw needn't show every extreme that they name: `sea_mask`: blocks of 128 points: the sea points of a block come first; some blocks are all land and some all sea. `upwind_lists`: A neighbour index below 8192 lies within 128 of the point's own index. A value 8192 + k names boundary point k, and k lies in k // 16 == (the point's index) // 128. `boundary_list`: boundary point k reads a coarse point j with (j % 1024) // 16 == k // 16.
All inputs are finite; a program needn't handle non-finite values.
Results may differ from a plain program's by a relative error of at most 0.0003.
Values sent between devices are 32-bit elements; how exact they have to be, the bound alone decides.
A program may use at most 64 MiB of HBM per device.

v0:
```python
import functools
import math

import jax
import jax.numpy as jnp
import numpy as np
from jax import lax
from jax.experimental import pallas as pl
from jax.experimental.pallas import tpu as pltpu
from jax.sharding import PartitionSpec as P

NDIR = 36
NFREQ = 32
BLOCK = 128
CHUNK = 3
NCHUNK = NDIR // CHUNK
MESH = pl.DeviceIdType.MESH


def kernel(
    n_pts,
    n_grp,
    trig_ref,
    spec_hbm,
    coarse_hbm,
    east_hbm,
    north_hbm,
    turn_hbm,
    kern_hbm,
    mask_hbm,
    lists_hbm,
    blist_hbm,
    out_ref,
    spec_v,
    winds_v,
    kern_v,
    mask_v,
    lists_v,
    blist_s,
    trig_s,
    coarse_v,
    coarse_n,
    lane_v,
    part_v,
    own,
    prv,
    nxt,
    load_sem,
    co_send,
    co_recv,
    send_sem,
    recv_sem,
):
    pos = lax.axis_index("pts")
    grp = lax.axis_index("grp")
    after = lax.rem(pos + 1, n_pts)
    before = lax.rem(pos + n_pts - 1, n_pts)
    group_points = mask_hbm.shape[1]
    ghosts = blist_hbm.shape[1]
    slots = coarse_hbm.shape[0]
    coarse_span = slots * n_pts

    here = pl.ds(pl.multiple_of(pos * BLOCK, BLOCK), BLOCK)
    loads = [
        pltpu.make_async_copy(spec_hbm, spec_v, load_sem.at[0]),
        pltpu.make_async_copy(coarse_hbm, coarse_v.at[grp], load_sem.at[1]),
        pltpu.make_async_copy(lists_hbm.at[:, here], lists_v, load_sem.at[2]),
        pltpu.make_async_copy(mask_hbm.at[:, here], mask_v, load_sem.at[3]),
        pltpu.make_async_copy(blist_hbm, blist_s, load_sem.at[4]),
        pltpu.make_async_copy(trig_ref, trig_s, load_sem.at[5]),
        pltpu.make_async_copy(east_hbm, winds_v.at[0], load_sem.at[6]),
        pltpu.make_async_copy(north_hbm, winds_v.at[1], load_sem.at[7]),
        pltpu.make_async_copy(turn_hbm, winds_v.at[2], load_sem.at[8]),
        pltpu.make_async_copy(kern_hbm, kern_v, load_sem.at[9]),
    ]
    for load in loads:
        load.start()

    barrier = pltpu.get_barrier_semaphore()
    pl.semaphore_signal(barrier, inc=1, device_id={"pts": after}, device_id_type=MESH)
    pl.semaphore_signal(barrier, inc=1, device_id={"pts": before}, device_id_type=MESH)
    for k in range(1, n_grp):
        peer = lax.rem(grp + k, n_grp)
        pl.semaphore_signal(barrier, inc=1, device_id={"grp": peer}, device_id_type=MESH)

    for load in loads[1:]:
        load.wait()
    lists = lists_v[...]
    shape = (4, BLOCK)
    slot = lists - (group_points + pos * ghosts)
    column = jnp.zeros(shape, jnp.int32)
    for k in range(ghosts):
        j = blist_s[0, k]
        col = lax.div(j, jnp.int32(coarse_span)) * slots + lax.rem(j, jnp.int32(slots))
        column = jnp.where(slot == k, col, column)
    rel = lists - (pos * BLOCK - BLOCK)
    is_far = lists >= group_points
    part = jnp.where(is_far, 3, lax.shift_right_arithmetic(rel, 7))
    lane = jnp.where(is_far, column, rel & 127)
    for r in range(4):
        lane_v[r] = jnp.broadcast_to(lane[r : r + 1], (NFREQ, BLOCK))
        part_v[r] = jnp.broadcast_to(part[r : r + 1], (NFREQ, BLOCK))

    maskf = jnp.broadcast_to(mask_v[...].astype(jnp.float32), (NFREQ, BLOCK))
    freq = lax.broadcasted_iota(jnp.int32, (NFREQ, BLOCK), 0).astype(jnp.float32)
    half_up = jnp.exp(freq * (0.5 * math.log(1.1)))
    courant = 0.65 * jnp.exp(freq * (-0.5 * math.log(1.1)))
    turn_factor = 0.5 + 0.5 * jnp.exp(freq * (-math.log(1.1)))

    loads[0].wait()
    comps = spec_v.shape[0]
    group_rows = 72

    def add_rows(i, acc):
        rows = spec_v[pl.ds(pl.multiple_of(i * group_rows, 8), group_rows), :]
        return acc + jnp.sum(rows.reshape(group_rows // 8, 8, BLOCK), axis=0)

    total = lax.fori_loop(0, comps // group_rows, add_rows, jnp.zeros((8, BLOCK), jnp.float32))
    etot = jnp.sum(total, axis=0, keepdims=True) * (1.0 / comps)
    diss = jnp.broadcast_to(0.3 * etot, (NFREQ, BLOCK)) * (0.5 + freq * (1.0 / NFREQ))

    pl.semaphore_wait(barrier, 2 + n_grp - 1)

    def coarse_copy(k):
        return pltpu.make_async_remote_copy(
            src_ref=coarse_hbm,
            dst_ref=coarse_v.at[grp],
            send_sem=co_send.at[k - 1],
            recv_sem=co_recv.at[k - 1],
            device_id={"grp": lax.rem(grp + k, n_grp)},
            device_id_type=MESH,
        )

    for k in range(1, n_grp):
        coarse_copy(k).start()

    def halo(step, c, way):
        rows = pl.ds(c * CHUNK, CHUNK)
        into = prv if way == 0 else nxt
        return pltpu.make_async_remote_copy(
            src_ref=own.at[step, rows],
            dst_ref=into.at[step, rows],
            send_sem=send_sem.at[step, way, c],
            recv_sem=recv_sem.at[step, way, c],
            device_id={"pts": after if way == 0 else before},
            device_id_type=MESH,
        )

    east = jnp.broadcast_to(winds_v[0], (NFREQ, BLOCK))
    north = jnp.broadcast_to(winds_v[1], (NFREQ, BLOCK))
    kern = kern_v[...]

    def source_chunk(c, carry):
        cells = [
            spec_v[pl.ds(c * CHUNK + i, NFREQ, stride=NDIR), :] for i in range(CHUNK)
        ]
        mixed = jnp.dot(
            kern,
            jnp.concatenate(cells, axis=1),
            precision=lax.Precision.HIGHEST,
            preferred_element_type=jnp.float32,
        )
        for i in range(CHUNK):
            d = c * CHUNK + i
            cell = cells[i]
            along = east * trig_s[0, d] + north * trig_s[1, d]
            grow = 0.1 * jnp.maximum(along * half_up - 1.0, 0.0)
            mix = mixed[:, i * BLOCK : (i + 1) * BLOCK]
            own[0, d] = maskf * (cell + cell * (grow - diss) + 0.2 * mix)
        halo(0, c, 0).start()
        halo(0, c, 1).start()
        return carry

    lax.fori_loop(0, NCHUNK, source_chunk, 0)

    for k in range(1, n_grp):
        coarse_copy(k).wait_recv()
    wide = coarse_v[...].reshape(n_grp * slots, comps)
    pad = jnp.zeros((BLOCK - n_grp * slots, BLOCK), jnp.float32)
    for t in range(comps // BLOCK):
        tile = jnp.concatenate([wide[:, t * BLOCK : (t + 1) * BLOCK], pad], axis=0)
        coarse_n[t * BLOCK : (t + 1) * BLOCK, :] = jnp.transpose(tile)

    def advect(step, c):
        quad = lax.div(c * CHUNK, 9)
        list_x = lax.rem(lax.div(quad + 1, 2), 2)
        list_y = 2 + lax.div(quad, 2)
        tables = []
        for which in (list_x, list_y):
            part_w = part_v[which]
            tables.append((lane_v[which], part_w == 0, part_w == 1, part_w == 2))
        results = []
        for i in range(CHUNK):
            d = c * CHUNK + i
            mine = own[step, d]
            sources = (
                prv[step, d],
                mine,
                nxt[step, d],
                coarse_n[pl.ds(d, NFREQ, stride=NDIR), :],
            )
            found = []
            for lane_w, p0, p1, p2 in tables:
                got = [
                    jnp.take_along_axis(source, lane_w, axis=1) for source in sources
                ]
                found.append(
                    jnp.where(p0, got[0], jnp.where(p1, got[1], jnp.where(p2, got[2], got[3])))
                )
            step_x = courant * trig_s[2, d]
            step_y = courant * trig_s[3, d]
            results.append(
                maskf * (mine - step_x * (mine - found[0]) - step_y * (mine - found[1]))
            )
        return results

    def first_chunk(c, carry):
        halo(0, c, 0).wait_recv()
        halo(0, c, 1).wait_recv()
        results = advect(0, c)
        for i in range(CHUNK):
            own[1, c * CHUNK + i] = results[i]
        halo(1, c, 0).start()
        halo(1, c, 1).start()
        return carry

    lax.fori_loop(0, NCHUNK, first_chunk, 0)

    rate = jnp.broadcast_to(winds_v[2], (NFREQ, BLOCK)) * turn_factor
    slow = jnp.abs(rate)
    turning_up = rate > 0

    def refract(d, low, high):
        mine = own[2, d]
        up = jnp.where(turning_up, own[2, low], own[2, high])
        out_ref[pl.ds(d, NFREQ, stride=NDIR), :] = maskf * (mine - slow * (mine - up))

    def second_chunk(c, carry):
        halo(1, c, 0).wait_recv()
        halo(1, c, 1).wait_recv()
        results = advect(1, c)
        for i in range(CHUNK):
            own[2, c * CHUNK + i] = results[i]
        return carry

    def second_and_turn(c, carry):
        second_chunk(c, carry)
        for i in range(CHUNK):
            d = c * CHUNK + i - 1
            refract(d, d - 1, d + 1)
        return carry

    second_chunk(0, 0)
    refract(1, 0, 2)
    lax.fori_loop(1, NCHUNK, second_and_turn, 0)
    refract(0, NDIR - 1, 1)
    refract(NDIR - 1, NDIR - 2, 0)

    def drain(c, carry):
        for step in range(2):
            for way in range(2):
                halo(step, c, way).wait_send()
        return carry

    lax.fori_loop(0, NCHUNK, drain, 0)
    for k in range(1, n_grp):
        coarse_copy(k).wait_send()


def trig_table():
    theta = 2.0 * math.pi * (np.arange(NDIR) + 0.5) / NDIR
    rows = [np.cos(theta), np.sin(theta), np.abs(np.cos(theta)), np.abs(np.sin(theta))]
    return np.stack(rows).astype(np.float32)


def shards(
    n_pts,
    n_grp,
    spectrum,
    coarse_spectra,
    wind_east,
    wind_north,
    refraction,
    freq_kernel,
    sea_mask,
    upwind_lists,
    boundary_list,
):
    comps = spectrum.shape[1]
    slots = coarse_spectra.shape[2]
    ghosts = boundary_list.shape[1]
    anyspace = pl.BlockSpec(memory_space=pl.ANY)
    block = (NDIR, NFREQ, BLOCK)
    out = pl.pallas_call(
        functools.partial(kernel, n_pts, n_grp),
        out_shape=jax.ShapeDtypeStruct((comps, BLOCK), jnp.float32),
        in_specs=[anyspace] * 10,
        out_specs=pl.BlockSpec(memory_space=pltpu.VMEM),
        scratch_shapes=[
            pltpu.VMEM((comps, BLOCK), jnp.float32),
            pltpu.VMEM((3, 1, BLOCK), jnp.float32),
            pltpu.VMEM((NFREQ, NFREQ), jnp.float32),
            pltpu.VMEM((1, BLOCK), jnp.int32),
            pltpu.VMEM((4, BLOCK), jnp.int32),
            pltpu.SMEM((1, ghosts), jnp.int32),
            pltpu.SMEM((4, NDIR), jnp.float32),
            pltpu.VMEM((n_grp, slots, comps), jnp.float32),
            pltpu.VMEM((comps, BLOCK), jnp.float32),
            pltpu.VMEM((4, NFREQ, BLOCK), jnp.int32),
            pltpu.VMEM((4, NFREQ, BLOCK), jnp.int32),
            pltpu.VMEM((3,) + block, jnp.float32),
            pltpu.VMEM((2,) + block, jnp.float32),
            pltpu.VMEM((2,) + block, jnp.float32),
            pltpu.SemaphoreType.DMA((10,)),
            pltpu.SemaphoreType.DMA((n_grp - 1,)),
            pltpu.SemaphoreType.DMA((n_grp - 1,)),
            pltpu.SemaphoreType.DMA((2, 2, NCHUNK)),
            pltpu.SemaphoreType.DMA((2, 2, NCHUNK)),
        ],
        compiler_params=pltpu.CompilerParams(
            collective_id=0, has_side_effects=True, vmem_limit_bytes=24 * 1024 * 1024
        ),
        name="wave_step",
    )(
        jnp.asarray(trig_table()),
        spectrum[0],
        jnp.transpose(coarse_spectra[0]),
        wind_east,
        wind_north,
        refraction,
        freq_kernel,
        sea_mask,
        upwind_lists[0],
        boundary_list,
    )
    return out[None]


def solution(mesh):
    placed = (
        P("grp", None, "pts"),
        P("grp", None, "pts"),
        P("grp", "pts"),
        P("grp", "pts"),
        P("grp", "pts"),
        P(),
        P("grp", None),
        P("grp", None, None),
        P("grp", "pts"),
    )
    return jax.shard_map(
        functools.partial(shards, mesh.shape["pts"], mesh.shape["grp"]),
        mesh=mesh,
        in_specs=placed,
        out_specs=P("grp", None, "pts"),
        check_vma=False,
    )
```

profile of v0, /device:TPU:2, one launch (start us, length us, event | category | flops | bytes accessed | tf_op | source)
XLA Modules:
  0.0 31.3 jit_solution(10736173236254733983)
XLA Ops:
  0.0 0.0 copy-start.9
  0.0 0.0 copy-start.5
  0.0 0.0 copy-start.6
  0.0 0.0 copy-start.7
  0.0 0.0 copy-start.8
  0.0 0.6 %copy-done.9 = s32[1,16]{1,0:T(1,128)S(1)} copy-done((s32[1,16]{1,0:T(1,128)S(1)}, s32[1,16]{1,0:T(1,128)}, u32[]{:S(2)}) %copy-start.9) | copy-done | bytes 88
  0.7 0.0 copy-done.5
  0.7 0.0 copy-done.6
  0.7 0.0 copy-done.7
  0.7 0.0 copy-done.8
  0.7 0.0 copy-start
  0.7 1.1 %copy-done = f32[1,1152,128]{2,1,0:T(8,128)S(1)} copy-done((f32[1,1152,128]{2,1,0:T(8,128)S(1)}, f32[1,1152,128]{2,1,0:T(8,128)}, u32[]{:S(2)}) %copy-start) | copy-done | bytes 589848
  1.8 0.0 copy-start.1
  1.8 0.9 %copy-done.1 = s32[1,4,8192]{2,1,0:T(4,128)S(1)} copy-done((s32[1,4,8192]{2,1,0:T(4,128)S(1)}, s32[1,4,8192]{2,1,0:T(4,128)}, u32[]{:S(2)}) %copy-start.1) | copy-done | bytes 131096
  2.7 0.0 copy-start.2
  2.7 0.9 %copy-done.2 = f32[1,1152,16]{1,2,0:T(8,128)S(1)} copy-done((f32[1,1152,16]{1,2,0:T(8,128)S(1)}, f32[1,1152,16]{1,2,0:T(8,128)}, u32[]{:S(2)}) %copy-start.2) | copy-done | bytes 73752
  3.6 0.0 copy-start.3
  3.6 0.8 %copy-done.3 = s32[1,8192]{1,0:T(1,128)S(1)} copy-done((s32[1,8192]{1,0:T(1,128)S(1)}, s32[1,8192]{1,0:T(1,128)}, u32[]{:S(2)}) %copy-start.3) | copy-done | bytes 32792
  4.3 0.0 copy-start.4
  4.3 0.7 %copy-done.4 = f32[32,32]{1,0:T(8,128)S(1)} copy-done((f32[32,32]{1,0:T(8,128)S(1)}, f32[32,32]{1,0:T(8,128)}, u32[]{:S(2)}) %copy-start.4) | copy-done | bytes 4120
  5.0 25.4 %wave_step.1 = f32[1152,128]{1,0:T(8,128)S(1)} custom-call(f32[4,36]{1,0:T(4,128)S(1)} %copy-done.5, f32[1152,128]{1,0:T(8,128)S(1)} %bitcast.7, f32[16,1152]{1,0:T(8,128)S(1)} %bitcast.9, f32[1,128]{1,0:T(1,128)S(1)} %copy-done.6, f32[1,128]{1,0:T(1,128)S(1)} %copy-done.7, f32[1,128]{1,0:T(1,128)S(1)} %copy-done.8, f32[32,32]{1,0:T(8,128)S(1)} %copy-done.4, ...), custom_call_target="tpu_custom_call" | custom-call | tf_op jit(solution)/shard_map/wave_step/pallas_call | solution.py:294
  30.5 0.8 %copy.12 = f32[1,1152,128]{2,1,0:T(8,128)} copy(f32[1,1152,128]{2,1,0:T(8,128)S(1)} %bitcast.6) | data formatting | bytes 1179648
Async XLA Ops:
  0.0 0.7 %copy-start.9 = (s32[1,16]{1,0:T(1,128)S(1)}, s32[1,16]{1,0:T(1,128)}, u32[]{:S(2)}) copy-start(s32[1,16]{1,0:T(1,128)} %blist_hbm.1) | copy-start | bytes 196
  0.0 0.7 %copy-start.5 = (f32[4,36]{1,0:T(4,128)S(1)}, f32[4,36]{1,0:T(4,128)}, u32[]{:S(2)}) copy-start(f32[4,36]{1,0:T(4,128)} %constant.2.clone.trig_ref) | copy-start | bytes 1732
  0.0 0.7 %copy-start.6 = (f32[1,128]{1,0:T(1,128)S(1)}, f32[1,128]{1,0:T(1,128)}, u32[]{:S(2)}) copy-start(f32[1,128]{1,0:T(1,128)} %east_hbm.1) | copy-start | bytes 1540
  0.0 0.7 %copy-start.7 = (f32[1,128]{1,0:T(1,128)S(1)}, f32[1,128]{1,0:T(1,128)}, u32[]{:S(2)}) copy-start(f32[1,128]{1,0:T(1,128)} %north_hbm.1) | copy-start | bytes 1540
  0.0 0.7 %copy-start.8 = (f32[1,128]{1,0:T(1,128)S(1)}, f32[1,128]{1,0:T(1,128)}, u32[]{:S(2)}) copy-start(f32[1,128]{1,0:T(1,128)} %turn_hbm.1) | copy-start | bytes 1540
  0.7 1.1 %copy-start = (f32[1,1152,128]{2,1,0:T(8,128)S(1)}, f32[1,1152,128]{2,1,0:T(8,128)}, u32[]{:S(2)}) copy-start(f32[1,1152,128]{2,1,0:T(8,128)} %param.10) | copy-start | bytes 1769476
  1.8 0.9 %copy-start.1 = (s32[1,4,8192]{2,1,0:T(4,128)S(1)}, s32[1,4,8192]{2,1,0:T(4,128)}, u32[]{:S(2)}) copy-start(s32[1,4,8192]{2,1,0:T(4,128)} %param.17) | copy-start | bytes 393220
  2.7 0.9 %copy-start.2 = (f32[1,1152,16]{1,2,0:T(8,128)S(1)}, f32[1,1152,16]{1,2,0:T(8,128)}, u32[]{:S(2)}) copy-start(f32[1,1152,16]{1,2,0:T(8,128)} %param.11) | copy-start | bytes 221188
  3.6 0.8 %copy-start.3 = (s32[1,8192]{1,0:T(1,128)S(1)}, s32[1,8192]{1,0:T(1,128)}, u32[]{:S(2)}) copy-start(s32[1,8192]{1,0:T(1,128)} %mask_hbm.1) | copy-start | bytes 98308
  4.3 0.7 %copy-start.4 = (f32[32,32]{1,0:T(8,128)S(1)}, f32[32,32]{1,0:T(8,128)}, u32[]{:S(2)}) copy-start(f32[32,32]{1,0:T(8,128)} %kern_hbm.1) | copy-start | bytes 12292
where the time goes:
time: 31.6 us; the launch traced here: 31.3 us
  Pallas kernels  25.4 us (80%)
  local copies, waits for them, and re-layouts  5.84 us (18%)
    pallas_call x1, Pallas kernels, shards(): pl.pallas_call(functools.partial(kernel, n_pts, n_grp), out_shape=jax.Sha...  25.4 us
    unnamed x21, local copies, waits for them, and re-layouts  5.84 us

commit v1 on v0

--- a/solution.py
+++ b/solution.py
@@ -40,8 +40,7 @@
     trig_s,
     coarse_v,
     coarse_n,
-    lane_v,
-    part_v,
+    pick_v,
     own,
     prv,
     nxt,
@@ -97,9 +96,7 @@
     is_far = lists >= group_points
     part = jnp.where(is_far, 3, lax.shift_right_arithmetic(rel, 7))
     lane = jnp.where(is_far, column, rel & 127)
-    for r in range(4):
-        lane_v[r] = jnp.broadcast_to(lane[r : r + 1], (NFREQ, BLOCK))
-        part_v[r] = jnp.broadcast_to(part[r : r + 1], (NFREQ, BLOCK))
+    place = part * BLOCK + lane
 
     maskf = jnp.broadcast_to(mask_v[...].astype(jnp.float32), (NFREQ, BLOCK))
     freq = lax.broadcasted_iota(jnp.int32, (NFREQ, BLOCK), 0).astype(jnp.float32)
@@ -148,16 +145,48 @@
 
     east = jnp.broadcast_to(winds_v[0], (NFREQ, BLOCK))
     north = jnp.broadcast_to(winds_v[1], (NFREQ, BLOCK))
-    kern = kern_v[...]
+    kern_f = kern_v[...]
+    kern_hi = kern_f.astype(jnp.bfloat16)
+    kern_lo = (kern_f - kern_hi.astype(jnp.float32)).astype(jnp.bfloat16)
+    kern = jnp.concatenate([kern_hi, kern_hi, kern_lo, kern_lo], axis=1)
+
+    def send_both(step, c):
+        @pl.when(pos < n_pts - 1)
+        def _():
+            halo(step, c, 0).start()
+
+        @pl.when(pos > 0)
+        def _():
+            halo(step, c, 1).start()
+
+    def await_both(step, c):
+        @pl.when(pos > 0)
+        def _():
+            halo(step, c, 0).wait_recv()
+
+        @pl.when(pos < n_pts - 1)
+        def _():
+            halo(step, c, 1).wait_recv()
+
+    def sent_both(step, c):
+        @pl.when(pos < n_pts - 1)
+        def _():
+            halo(step, c, 0).wait_send()
+
+        @pl.when(pos > 0)
+        def _():
+            halo(step, c, 1).wait_send()
 
     def source_chunk(c, carry):
         cells = [
             spec_v[pl.ds(c * CHUNK + i, NFREQ, stride=NDIR), :] for i in range(CHUNK)
         ]
+        wide = jnp.concatenate(cells, axis=1)
+        wide_hi = wide.astype(jnp.bfloat16)
+        wide_lo = (wide - wide_hi.astype(jnp.float32)).astype(jnp.bfloat16)
         mixed = jnp.dot(
             kern,
-            jnp.concatenate(cells, axis=1),
-            precision=lax.Precision.HIGHEST,
+            jnp.concatenate([wide_hi, wide_lo, wide_hi, wide_lo], axis=0),
             preferred_element_type=jnp.float32,
         )
         for i in range(CHUNK):
@@ -167,11 +196,30 @@
             grow = 0.1 * jnp.maximum(along * half_up - 1.0, 0.0)
             mix = mixed[:, i * BLOCK : (i + 1) * BLOCK]
             own[0, d] = maskf * (cell + cell * (grow - diss) + 0.2 * mix)
-        halo(0, c, 0).start()
-        halo(0, c, 1).start()
+        send_both(0, c)
         return carry
 
     lax.fori_loop(0, NCHUNK, source_chunk, 0)
+
+    def clear(into):
+        def clear_one(d, carry):
+            for step in range(2):
+                into[step, d] = jnp.zeros((NFREQ, BLOCK), jnp.float32)
+            return carry
+
+        lax.fori_loop(0, NDIR, clear_one, 0)
+
+    @pl.when(pos == 0)
+    def _():
+        clear(prv)
+
+    @pl.when(pos == n_pts - 1)
+    def _():
+        clear(nxt)
+
+    window = lax.broadcasted_iota(jnp.int32, (4 * BLOCK, BLOCK), 0)
+    for r in range(4):
+        pick_v[r] = jnp.where(window == place[r : r + 1], 1.0, 0.0).astype(jnp.bfloat16)
 
     for k in range(1, n_grp):
         coarse_copy(k).wait_recv()
@@ -185,43 +233,49 @@
         quad = lax.div(c * CHUNK, 9)
         list_x = lax.rem(lax.div(quad + 1, 2), 2)
         list_y = 2 + lax.div(quad, 2)
-        tables = []
-        for which in (list_x, list_y):
-            part_w = part_v[which]
-            tables.append((lane_v[which], part_w == 0, part_w == 1, part_w == 2))
+        picks = jnp.concatenate([pick_v[list_x], pick_v[list_y]], axis=1)
+        mine = [own[step, c * CHUNK + i] for i in range(CHUNK)]
+        rows = CHUNK * NFREQ
+        here_rows = pl.ds(c * CHUNK, CHUNK)
+        windows = jnp.concatenate(
+            [
+                prv[step, here_rows].reshape(rows, BLOCK),
+                own[step, here_rows].reshape(rows, BLOCK),
+                nxt[step, here_rows].reshape(rows, BLOCK),
+                jnp.concatenate(
+                    [
+                        coarse_n[pl.ds(c * CHUNK + i, NFREQ, stride=NDIR), :]
+                        for i in range(CHUNK)
+                    ],
+                    axis=0,
+                ),
+            ],
+            axis=1,
+        )
+        high = windows.astype(jnp.bfloat16)
+        low = (windows - high.astype(jnp.float32)).astype(jnp.bfloat16)
+        found = jnp.dot(high, picks, preferred_element_type=jnp.float32) + jnp.dot(
+            low, picks, preferred_element_type=jnp.float32
+        )
         results = []
         for i in range(CHUNK):
             d = c * CHUNK + i
-            mine = own[step, d]
-            sources = (
-                prv[step, d],
-                mine,
-                nxt[step, d],
-                coarse_n[pl.ds(d, NFREQ, stride=NDIR), :],
-            )
-            found = []
-            for lane_w, p0, p1, p2 in tables:
-                got = [
-                    jnp.take_along_axis(source, lane_w, axis=1) for source in sources
-                ]
-                found.append(
-                    jnp.where(p0, got[0], jnp.where(p1, got[1], jnp.where(p2, got[2], got[3])))
-                )
+            cell = mine[i]
+            from_x = found[i * NFREQ : (i + 1) * NFREQ, :BLOCK]
+            from_y = found[i * NFREQ : (i + 1) * NFREQ, BLOCK:]
             step_x = courant * trig_s[2, d]
             step_y = courant * trig_s[3, d]
             results.append(
-                maskf * (mine - step_x * (mine - found[0]) - step_y * (mine - found[1]))
+                maskf * (cell - step_x * (cell - from_x) - step_y * (cell - from_y))
             )
         return results
 
     def first_chunk(c, carry):
-        halo(0, c, 0).wait_recv()
-        halo(0, c, 1).wait_recv()
+        await_both(0, c)
         results = advect(0, c)
         for i in range(CHUNK):
             own[1, c * CHUNK + i] = results[i]
-        halo(1, c, 0).start()
-        halo(1, c, 1).start()
+        send_both(1, c)
         return carry
 
     lax.fori_loop(0, NCHUNK, first_chunk, 0)
@@ -236,8 +290,7 @@
         out_ref[pl.ds(d, NFREQ, stride=NDIR), :] = maskf * (mine - slow * (mine - up))
 
     def second_chunk(c, carry):
-        halo(1, c, 0).wait_recv()
-        halo(1, c, 1).wait_recv()
+        await_both(1, c)
         results = advect(1, c)
         for i in range(CHUNK):
             own[2, c * CHUNK + i] = results[i]
@@ -258,8 +311,7 @@
 
     def drain(c, carry):
         for step in range(2):
-            for way in range(2):
-                halo(step, c, way).wait_send()
+            sent_both(step, c)
         return carry
 
     lax.fori_loop(0, NCHUNK, drain, 0)
@@ -306,8 +358,7 @@
             pltpu.SMEM((4, NDIR), jnp.float32),
             pltpu.VMEM((n_grp, slots, comps), jnp.float32),
             pltpu.VMEM((comps, BLOCK), jnp.float32),
-            pltpu.VMEM((4, NFREQ, BLOCK), jnp.int32),
-            pltpu.VMEM((4, NFREQ, BLOCK), jnp.int32),
+            pltpu.VMEM((4, 4 * BLOCK, BLOCK), jnp.bfloat16),
             pltpu.VMEM((3,) + block, jnp.float32),
             pltpu.VMEM((2,) + block, jnp.float32),
             pltpu.VMEM((2,) + block, jnp.float32),
@@ -321,7 +372,7 @@
             collective_id=0, has_side_effects=True, vmem_limit_bytes=24 * 1024 * 1024
         ),
         name="wave_step",
-    )(
+    )(*[pltpu.with_memory_space_constraint(a, pltpu.HBM) for a in (
         jnp.asarray(trig_table()),
         spectrum[0],
         jnp.transpose(coarse_spectra[0]),
@@ -332,7 +383,7 @@
         sea_mask,
         upwind_lists[0],
         boundary_list,
-    )
+    )])
     return out[None]
 
 

time: 31.6 us -> 24.6 us (0.78)
  the two profiles are of different devices: /device:TPU:2 before, /device:TPU:24 now
where the time goes in v1:
time: 24.6 us; the launch traced here: 24.5 us
  Pallas kernels  23.7 us (96%)
  local copies, waits for them, and re-layouts  0.82 us (3%)
    pallas_call x1, Pallas kernels, shards(): pl.pallas_call(functools.partial(kernel, n_pts, n_grp), out_shape=jax.Sha...  23.7 us
    unnamed x1, local copies, waits for them, and re-layouts  0.82 us

profile of v1, /device:TPU:24, one launch (start us, length us, event | category | flops | bytes accessed | tf_op | source)
XLA Modules:
  0.0 24.5 jit_solution(17475686414830523649)
XLA Ops:
  0.0 23.7 %wave_step.1 = f32[1152,128]{1,0:T(8,128)S(1)} custom-call(f32[4,36]{1,0:T(4,128)} %constant.2.clone.trig_ref, f32[1152,128]{1,0:T(8,128)} %bitcast.7, f32[16,1152]{1,0:T(8,128)} %bitcast.9, f32[1,128]{1,0:T(1,128)} %east_hbm.1, f32[1,128]{1,0:T(1,128)} %north_hbm.1, f32[1,128]{1,0:T(1,128)} %turn_hbm.1, f32[32,32]{1,0:T(8,128)} %kern_hbm.1, ...), custom_call_target="tpu_custom_call" | custom-call | tf_op jit(solution)/shard_map/wave_step/pallas_call | solution.py:346
  23.7 0.8 %copy.12 = f32[1,1152,128]{2,1,0:T(8,128)} copy(f32[1,1152,128]{2,1,0:T(8,128)S(1)} %bitcast.6) | data formatting | bytes 1179648

commit v2 on v1

v2 whole, which is shorter than its diff:
```python
import functools
import math

import jax
import jax.numpy as jnp
import numpy as np
from jax import lax
from jax.experimental import pallas as pl
from jax.experimental.pallas import tpu as pltpu
from jax.sharding import PartitionSpec as P

NDIR = 36
NFREQ = 32
BLOCK = 128
QUAD = NDIR // 4
PIECE = 3
CUTS = ((0, 3, 9, 18, 27, 36), (0, 9, 18, 27, 33, 36))
LOADS = 4
HANDS = (
    (0, 0, 1),
    (1, 1, 2),
    (1, 1, 3),
    (1, 1, 0),
    (2, 2, 3),
    (2, 2, 1),
    (2, 2, 0),
    (3, 3, 2),
    (3, 3, 1),
    (3, 3, 0),
    (0, 1, 2),
    (0, 1, 3),
)
GREETED = (1, 3)
ARRIVALS = ((1, 2, 3), (0, 2, 3), (1, 3, 0), (2, 1, 0))
MESH = pl.DeviceIdType.MESH


def kernel(
    n_pts,
    n_grp,
    trig_ref,
    spec_hbm,
    coarse_hbm,
    east_hbm,
    north_hbm,
    turn_hbm,
    kern_hbm,
    mask_hbm,
    lists_hbm,
    blist_hbm,
    out_ref,
    spec_v,
    winds_v,
    kern_v,
    mask_v,
    lists_v,
    blist_s,
    trig_s,
    coarse_v,
    coarse_n,
    pick_v,
    own,
    prv,
    nxt,
    load_sem,
    spec_sem,
    co_send,
    co_recv,
    send_sem,
    recv_sem,
):
    pos = lax.axis_index("pts")
    grp = lax.axis_index("grp")
    after = lax.rem(pos + 1, n_pts)
    before = lax.rem(pos + n_pts - 1, n_pts)
    has_before = pos > 0
    has_after = pos < n_pts - 1
    group_points = mask_hbm.shape[1]
    ghosts = blist_hbm.shape[1]
    slots, comps = coarse_hbm.shape
    coarse_span = slots * n_pts

    barrier = pltpu.get_barrier_semaphore()

    @pl.when(has_before)
    def _():
        pl.semaphore_signal(barrier, inc=1, device_id={"pts": before}, device_id_type=MESH)

    @pl.when(has_after)
    def _():
        pl.semaphore_signal(barrier, inc=1, device_id={"pts": after}, device_id_type=MESH)

    for g in range(n_grp):
        for owner, sender, to in HANDS:
            if to == g and owner == sender:

                @pl.when(grp == to)
                def _():
                    pl.semaphore_signal(
                        barrier, inc=1, device_id={"grp": sender}, device_id_type=MESH
                    )

    here = pl.ds(pl.multiple_of(pos * BLOCK, BLOCK), BLOCK)
    rows = comps // LOADS
    spec_loads = [
        pltpu.make_async_copy(
            spec_hbm.at[pl.ds(i * rows, rows)], spec_v.at[pl.ds(i * rows, rows)], spec_sem.at[i]
        )
        for i in range(LOADS)
    ]
    early_loads = [
        pltpu.make_async_copy(trig_ref, trig_s, load_sem.at[0]),
        pltpu.make_async_copy(east_hbm, winds_v.at[0], load_sem.at[1]),
        pltpu.make_async_copy(north_hbm, winds_v.at[1], load_sem.at[2]),
        pltpu.make_async_copy(kern_hbm, kern_v, load_sem.at[3]),
        pltpu.make_async_copy(mask_hbm.at[:, here], mask_v, load_sem.at[4]),
        pltpu.make_async_copy(coarse_hbm, coarse_v.at[grp], load_sem.at[5]),
    ]
    late_loads = [
        pltpu.make_async_copy(lists_hbm.at[:, here], lists_v, load_sem.at[6]),
        pltpu.make_async_copy(blist_hbm, blist_s, load_sem.at[7]),
        pltpu.make_async_copy(turn_hbm, winds_v.at[2], load_sem.at[8]),
    ]
    for load in spec_loads + early_loads + late_loads:
        load.start()

    freq = lax.broadcasted_iota(jnp.int32, (NFREQ, BLOCK), 0).astype(jnp.float32)
    half_up = jnp.exp(freq * (0.5 * math.log(1.1)))
    courant = 0.65 * jnp.exp(freq * (-0.5 * math.log(1.1)))
    turn_factor = 0.5 + 0.5 * jnp.exp(freq * (-math.log(1.1)))

    for load in early_loads:
        load.wait()
    maskf = jnp.broadcast_to(mask_v[...].astype(jnp.float32), (NFREQ, BLOCK))
    east = jnp.broadcast_to(winds_v[0], (NFREQ, BLOCK))
    north = jnp.broadcast_to(winds_v[1], (NFREQ, BLOCK))
    kern_f = kern_v[...]
    kern_hi = kern_f.astype(jnp.bfloat16)
    kern_lo = (kern_f - kern_hi.astype(jnp.float32)).astype(jnp.bfloat16)
    kern = jnp.concatenate([kern_hi, kern_hi, kern_lo, kern_lo], axis=1)

    total = jnp.zeros((8, BLOCK), jnp.float32)
    for i in range(LOADS):
        spec_loads[i].wait()
        part = spec_v[i * rows : (i + 1) * rows, :].reshape(rows // 8, 8, BLOCK)
        total = total + jnp.sum(part, axis=0)
    etot = jnp.sum(total, axis=0, keepdims=True) * (1.0 / comps)
    diss = jnp.broadcast_to(0.3 * etot, (NFREQ, BLOCK)) * (0.5 + freq * (1.0 / NFREQ))

    def halo(step, c, way):
        first, end = CUTS[step][c], CUTS[step][c + 1]
        into = prv if way == 0 else nxt
        return pltpu.make_async_remote_copy(
            src_ref=own.at[step, pl.ds(first, end - first)],
            dst_ref=into.at[step, pl.ds(first, end - first)],
            send_sem=send_sem.at[step, way, c],
            recv_sem=recv_sem.at[step, way, c],
            device_id={"pts": after if way == 0 else before},
            device_id_type=MESH,
        )

    def send_both(step, c):
        @pl.when(has_after)
        def _():
            halo(step, c, 0).start()

        @pl.when(has_before)
        def _():
            halo(step, c, 1).start()

    def await_both(step, c):
        @pl.when(has_before)
        def _():
            halo(step, c, 0).wait_recv()

        @pl.when(has_after)
        def _():
            halo(step, c, 1).wait_recv()

    def sent_both(step, c):
        @pl.when(has_after)
        def _():
            halo(step, c, 0).wait_send()

        @pl.when(has_before)
        def _():
            halo(step, c, 1).wait_send()

    def hand(owner, to):
        own_block = coarse_v.at[owner]
        return pltpu.make_async_remote_copy(
            src_ref=own_block,
            dst_ref=own_block,
            send_sem=co_send.at[owner, to],
            recv_sem=co_recv.at[owner],
            device_id={"grp": to},
            device_id_type=MESH,
        )

    def source(first):
        cells = [spec_v[pl.ds(first + i, NFREQ, stride=NDIR), :] for i in range(PIECE)]
        wide = jnp.concatenate(cells, axis=1)
        wide_hi = wide.astype(jnp.bfloat16)
        wide_lo = (wide - wide_hi.astype(jnp.float32)).astype(jnp.bfloat16)
        mixed = jnp.dot(
            kern,
            jnp.concatenate([wide_hi, wide_lo, wide_hi, wide_lo], axis=0),
            preferred_element_type=jnp.float32,
        )
        for i in range(PIECE):
            d = first + i
            cell = cells[i]
            along = east * trig_s[0, d] + north * trig_s[1, d]
            grow = 0.1 * jnp.maximum(along * half_up - 1.0, 0.0)
            mix = mixed[:, i * BLOCK : (i + 1) * BLOCK]
            own[0, d] = maskf * (cell + cell * (grow - diss) + 0.2 * mix)

    parts = len(CUTS[0]) - 1
    for c in range(parts):
        for first in range(CUTS[0][c], CUTS[0][c + 1], PIECE):
            source(first)
        if c == 0:

            greeted = jnp.where(grp == 0, GREETED[0], GREETED[1])
            greeted += jnp.where(has_before, 1, 0) + jnp.where(has_after, 1, 0)
            pl.semaphore_wait(barrier, greeted)

            for g in range(n_grp):

                @pl.when(grp == g)
                def _():
                    for owner, sender, to in HANDS:
                        if owner == sender == g:
                            hand(owner, to).start()

        send_both(0, c)
    for load in late_loads:
        load.wait()
    lists = lists_v[...]
    shape = (4, BLOCK)
    slot = lists - (group_points + pos * ghosts)
    column = jnp.zeros(shape, jnp.int32)
    for k in range(ghosts):
        j = blist_s[0, k]
        col = lax.div(j, jnp.int32(coarse_span)) * slots + lax.rem(j, jnp.int32(slots))
        column = jnp.where(slot == k, col, column)
    rel = lists - (pos * BLOCK - BLOCK)
    is_far = lists >= group_points
    place = jnp.where(is_far, 3 * BLOCK + column, rel)

    window = lax.broadcasted_iota(jnp.int32, (4 * BLOCK, BLOCK), 0)
    for r in range(4):
        pick_v[r] = jnp.where(window == place[r : r + 1], 1.0, 0.0).astype(jnp.bfloat16)

    def clear(into):
        def clear_one(d, carry):
            for step in range(2):
                into[step, d] = jnp.zeros((NFREQ, BLOCK), jnp.float32)
            return carry

        lax.fori_loop(0, NDIR, clear_one, 0)

    @pl.when(pos == 0)
    def _():
        clear(prv)

    @pl.when(pos == n_pts - 1)
    def _():
        clear(nxt)

    for g in range(n_grp):

        @pl.when(grp == g)
        def _():
            for owner in ARRIVALS[g]:
                hand(owner, g).wait_recv()
                for relayed, sender, to in HANDS:
                    if relayed == owner and sender == g:
                        hand(owner, to).start()

    stacked = coarse_v[...].reshape(n_grp * slots, comps)
    pad = jnp.zeros((BLOCK - n_grp * slots, BLOCK), jnp.float32)
    for t in range(comps // BLOCK):
        tile = jnp.concatenate([stacked[:, t * BLOCK : (t + 1) * BLOCK], pad], axis=0)
        coarse_n[t * BLOCK : (t + 1) * BLOCK, :] = jnp.transpose(tile)

    def advect(step, first, end):
        quad = first // QUAD
        picks = jnp.concatenate(
            [pick_v[(quad + 1) // 2 % 2], pick_v[2 + quad // 2]], axis=1
        )
        cells = (end - first) * NFREQ
        windows = jnp.concatenate(
            [
                prv[step, first:end].reshape(cells, BLOCK),
                own[step, first:end].reshape(cells, BLOCK),
                nxt[step, first:end].reshape(cells, BLOCK),
                jnp.concatenate(
                    [coarse_n[pl.ds(d, NFREQ, stride=NDIR), :] for d in range(first, end)],
                    axis=0,
                ),
            ],
            axis=1,
        )
        high = windows.astype(jnp.bfloat16)
        low = (windows - high.astype(jnp.float32)).astype(jnp.bfloat16)
        both = jnp.dot(
            jnp.concatenate([high, low], axis=0), picks, preferred_element_type=jnp.float32
        )
        found = both[:cells] + both[cells:]
        for d in range(first, end):
            cell = own[step, d]
            at = (d - first) * NFREQ
            from_x = found[at : at + NFREQ, :BLOCK]
            from_y = found[at : at + NFREQ, BLOCK:]
            step_x = courant * trig_s[2, d]
            step_y = courant * trig_s[3, d]
            own[step + 1, d] = maskf * (
                cell - step_x * (cell - from_x) - step_y * (cell - from_y)
            )

    got = sent = 0
    for first in range(0, NDIR, QUAD):
        while got < parts and CUTS[0][got] < first + QUAD:
            await_both(0, got)
            got += 1
        advect(0, first, first + QUAD)
        while sent < parts and CUTS[1][sent + 1] <= first + QUAD:
            send_both(1, sent)
            sent += 1

    rate = jnp.broadcast_to(winds_v[2], (NFREQ, BLOCK)) * turn_factor
    slow = jnp.abs(rate)
    turning_up = rate > 0

    def refract(d):
        mine = own[2, d]
        up = jnp.where(turning_up, own[2, (d - 1) % NDIR], own[2, (d + 1) % NDIR])
        out_ref[pl.ds(d, NFREQ, stride=NDIR), :] = maskf * (mine - slow * (mine - up))

    done = 1
    for c in range(parts):
        await_both(1, c)
        advect(1, CUTS[1][c], CUTS[1][c + 1])
        while done < CUTS[1][c + 1] - 1:
            refract(done)
            done += 1
    refract(NDIR - 1)
    refract(0)

    for step in range(2):
        for c in range(parts):
            sent_both(step, c)
    for g in range(n_grp):

        @pl.when(grp == g)
        def _():
            for owner, sender, to in HANDS:
                if sender == g:
                    hand(owner, to).wait_send()


def trig_table():
    theta = 2.0 * math.pi * (np.arange(NDIR) + 0.5) / NDIR
    rows = [np.cos(theta), np.sin(theta), np.abs(np.cos(theta)), np.abs(np.sin(theta))]
    return np.stack(rows).astype(np.float32)


def shards(
    n_pts,
    n_grp,
    spectrum,
    coarse_spectra,
    wind_east,
    wind_north,
    refraction,
    freq_kernel,
    sea_mask,
    upwind_lists,
    boundary_list,
):
    comps = spectrum.shape[1]
    slots = coarse_spectra.shape[2]
    ghosts = boundary_list.shape[1]
    anyspace = pl.BlockSpec(memory_space=pl.ANY)
    block = (NDIR, NFREQ, BLOCK)
    out = pl.pallas_call(
        functools.partial(kernel, n_pts, n_grp),
        out_shape=jax.ShapeDtypeStruct((comps, BLOCK), jnp.float32),
        in_specs=[anyspace] * 10,
        out_specs=pl.BlockSpec(memory_space=pltpu.VMEM),
        scratch_shapes=[
            pltpu.VMEM((comps, BLOCK), jnp.float32),
            pltpu.VMEM((3, 1, BLOCK), jnp.float32),
            pltpu.VMEM((NFREQ, NFREQ), jnp.float32),
            pltpu.VMEM((1, BLOCK), jnp.int32),
            pltpu.VMEM((4, BLOCK), jnp.int32),
            pltpu.SMEM((1, ghosts), jnp.int32),
            pltpu.SMEM((4, NDIR), jnp.float32),
            pltpu.VMEM((n_grp, slots, comps), jnp.float32),
            pltpu.VMEM((comps, BLOCK), jnp.float32),
            pltpu.VMEM((4, 4 * BLOCK, BLOCK), jnp.bfloat16),
            pltpu.VMEM((3,) + block, jnp.float32),
            pltpu.VMEM((2,) + block, jnp.float32),
            pltpu.VMEM((2,) + block, jnp.float32),
            pltpu.SemaphoreType.DMA((9,)),
            pltpu.SemaphoreType.DMA((LOADS,)),
            pltpu.SemaphoreType.DMA((n_grp, n_grp)),
            pltpu.SemaphoreType.DMA((n_grp,)),
            pltpu.SemaphoreType.DMA((2, 2, len(CUTS[0]) - 1)),
            pltpu.SemaphoreType.DMA((2, 2, len(CUTS[0]) - 1)),
        ],
        compiler_params=pltpu.CompilerParams(
            collective_id=0, has_side_effects=True, vmem_limit_bytes=24 * 1024 * 1024
        ),
        name="wave_step",
    )(*[pltpu.with_memory_space_constraint(a, pltpu.HBM) for a in (
        jnp.asarray(trig_table()),
        spectrum[0],
        jnp.transpose(coarse_spectra[0]),
        wind_east,
        wind_north,
        refraction,
        freq_kernel,
        sea_mask,
        upwind_lists[0],
        boundary_list,
    )])
    return out[None]


def solution(mesh):
    placed = (
        P("grp", None, "pts"),
        P("grp", None, "pts"),
        P("grp", "pts"),
        P("grp", "pts"),
        P("grp", "pts"),
        P(),
        P("grp", None),
        P("grp", None, None),
        P("grp", "pts"),
    )
    return jax.shard_map(
        functools.partial(shards, mesh.shape["pts"], mesh.shape["grp"]),
        mesh=mesh,
        in_specs=placed,
        out_specs=P("grp", None, "pts"),
        check_vma=False,
    )
```

time: 24.6 us -> 23.1 us (0.939)
  the two profiles are of different devices: /device:TPU:24 before, /device:TPU:30 now
where the time goes in v2:
time: 23.1 us; the launch traced here: 23 us
  Pallas kernels  22.2 us (96%)
  local copies, waits for them, and re-layouts  0.82 us (4%)
    pallas_call x1, Pallas kernels, shards(): pl.pallas_call(functools.partial(kernel, n_pts, n_grp), out_shape=jax.Sha...  22.2 us
    unnamed x1, local copies, waits for them, and re-layouts  0.82 us

profile of v2, /device:TPU:30, one launch (start us, length us, event | category | flops | bytes accessed | tf_op | source)
XLA Modules:
  0.0 23.0 jit_solution(6298652622753579920)
XLA Ops:
  0.0 22.2 %wave_step.1 = f32[1152,128]{1,0:T(8,128)S(1)} custom-call(f32[4,36]{1,0:T(4,128)} %constant.2.clone.trig_ref, f32[1152,128]{1,0:T(8,128)} %bitcast.7, f32[16,1152]{1,0:T(8,128)} %bitcast.9, f32[1,128]{1,0:T(1,128)} %east_hbm.1, f32[1,128]{1,0:T(1,128)} %north_hbm.1, f32[1,128]{1,0:T(1,128)} %turn_hbm.1, f32[32,32]{1,0:T(8,128)} %kern_hbm.1, ...), custom_call_target="tpu_custom_call" | custom-call | tf_op jit(solution)/shard_map/wave_step/pallas_call | solution.py:387
  22.2 0.8 %copy.12 = f32[1,1152,128]{2,1,0:T(8,128)} copy(f32[1,1152,128]{2,1,0:T(8,128)S(1)} %bitcast.6) | data formatting | bytes 1179648

commit v3 on v2

--- a/solution.py
+++ b/solution.py
@@ -16,22 +16,7 @@
 PIECE = 3
 CUTS = ((0, 3, 9, 18, 27, 36), (0, 9, 18, 27, 33, 36))
 LOADS = 4
-HANDS = (
-    (0, 0, 1),
-    (1, 1, 2),
-    (1, 1, 3),
-    (1, 1, 0),
-    (2, 2, 3),
-    (2, 2, 1),
-    (2, 2, 0),
-    (3, 3, 2),
-    (3, 3, 1),
-    (3, 3, 0),
-    (0, 1, 2),
-    (0, 1, 3),
-)
-GREETED = (1, 3)
-ARRIVALS = ((1, 2, 3), (0, 2, 3), (1, 3, 0), (2, 1, 0))
+EAGER = 2
 MESH = pl.DeviceIdType.MESH
 
 
@@ -64,6 +49,7 @@
     nxt,
     load_sem,
     spec_sem,
+    hello,
     co_send,
     co_recv,
     send_sem,
@@ -90,15 +76,11 @@
     def _():
         pl.semaphore_signal(barrier, inc=1, device_id={"pts": after}, device_id_type=MESH)
 
-    for g in range(n_grp):
-        for owner, sender, to in HANDS:
-            if to == g and owner == sender:
-
-                @pl.when(grp == to)
-                def _():
-                    pl.semaphore_signal(
-                        barrier, inc=1, device_id={"grp": sender}, device_id_type=MESH
-                    )
+    for k in range(1, n_grp):
+
+        @pl.when(grp < k)
+        def _():
+            pl.semaphore_signal(barrier, inc=1, device_id={"grp": k}, device_id_type=MESH)
 
     here = pl.ds(pl.multiple_of(pos * BLOCK, BLOCK), BLOCK)
     rows = comps // LOADS
@@ -114,15 +96,56 @@
         pltpu.make_async_copy(north_hbm, winds_v.at[1], load_sem.at[2]),
         pltpu.make_async_copy(kern_hbm, kern_v, load_sem.at[3]),
         pltpu.make_async_copy(mask_hbm.at[:, here], mask_v, load_sem.at[4]),
-        pltpu.make_async_copy(coarse_hbm, coarse_v.at[grp], load_sem.at[5]),
     ]
     late_loads = [
+        pltpu.make_async_copy(coarse_hbm, coarse_v.at[grp], load_sem.at[5]),
         pltpu.make_async_copy(lists_hbm.at[:, here], lists_v, load_sem.at[6]),
         pltpu.make_async_copy(blist_hbm, blist_s, load_sem.at[7]),
         pltpu.make_async_copy(turn_hbm, winds_v.at[2], load_sem.at[8]),
     ]
     for load in spec_loads + early_loads + late_loads:
         load.start()
+
+    def hand(to):
+        return pltpu.make_async_remote_copy(
+            src_ref=coarse_hbm,
+            dst_ref=coarse_v.at[grp],
+            send_sem=co_send.at[to],
+            recv_sem=co_recv.at[grp],
+            device_id={"grp": to},
+            device_id_type=MESH,
+        )
+
+    def arrival(owner):
+        return pltpu.make_async_remote_copy(
+            src_ref=coarse_v.at[owner],
+            dst_ref=coarse_v.at[owner],
+            send_sem=co_send.at[owner],
+            recv_sem=co_recv.at[owner],
+            device_id={"grp": owner},
+            device_id_type=MESH,
+        )
+
+    def meet():
+        greeted = grp + jnp.where(has_before, 1, 0) + jnp.where(has_after, 1, 0)
+        pl.semaphore_wait(barrier, greeted)
+        for k in range(n_grp - 1):
+
+            @pl.when(grp > k)
+            def _():
+                pl.semaphore_signal(
+                    hello.at[grp], inc=1, device_id={"grp": k}, device_id_type=MESH
+                )
+
+        for k in range(n_grp - 1):
+
+            @pl.when((grp > k) & ((k != 0) | (grp != 2)))
+            def _():
+                hand(k).start()
+
+    @pl.when(grp >= EAGER)
+    def _():
+        meet()
 
     freq = lax.broadcasted_iota(jnp.int32, (NFREQ, BLOCK), 0).astype(jnp.float32)
     half_up = jnp.exp(freq * (0.5 * math.log(1.1)))
@@ -186,17 +209,6 @@
         def _():
             halo(step, c, 1).wait_send()
 
-    def hand(owner, to):
-        own_block = coarse_v.at[owner]
-        return pltpu.make_async_remote_copy(
-            src_ref=own_block,
-            dst_ref=own_block,
-            send_sem=co_send.at[owner, to],
-            recv_sem=co_recv.at[owner],
-            device_id={"grp": to},
-            device_id_type=MESH,
-        )
-
     def source(first):
         cells = [spec_v[pl.ds(first + i, NFREQ, stride=NDIR), :] for i in range(PIECE)]
         wide = jnp.concatenate(cells, axis=1)
@@ -221,19 +233,22 @@
             source(first)
         if c == 0:
 
-            greeted = jnp.where(grp == 0, GREETED[0], GREETED[1])
-            greeted += jnp.where(has_before, 1, 0) + jnp.where(has_after, 1, 0)
-            pl.semaphore_wait(barrier, greeted)
-
-            for g in range(n_grp):
-
-                @pl.when(grp == g)
-                def _():
-                    for owner, sender, to in HANDS:
-                        if owner == sender == g:
-                            hand(owner, to).start()
+            @pl.when(grp < EAGER)
+            def _():
+                meet()
 
         send_both(0, c)
+    @pl.when(grp == 2)
+    def _():
+        hand(0).start()
+
+    for k in range(1, n_grp):
+
+        @pl.when(grp < k)
+        def _():
+            pl.semaphore_wait(hello.at[k], 1)
+            hand(k).start()
+
     for load in late_loads:
         load.wait()
     lists = lists_v[...]
@@ -268,15 +283,11 @@
     def _():
         clear(nxt)
 
-    for g in range(n_grp):
-
-        @pl.when(grp == g)
-        def _():
-            for owner in ARRIVALS[g]:
-                hand(owner, g).wait_recv()
-                for relayed, sender, to in HANDS:
-                    if relayed == owner and sender == g:
-                        hand(owner, to).start()
+    for k in range(n_grp):
+
+        @pl.when(grp != k)
+        def _():
+            arrival(k).wait_recv()
 
     stacked = coarse_v[...].reshape(n_grp * slots, comps)
     pad = jnp.zeros((BLOCK - n_grp * slots, BLOCK), jnp.float32)
@@ -351,13 +362,11 @@
     for step in range(2):
         for c in range(parts):
             sent_both(step, c)
-    for g in range(n_grp):
-
-        @pl.when(grp == g)
-        def _():
-            for owner, sender, to in HANDS:
-                if sender == g:
-                    hand(owner, to).wait_send()
+    for k in range(n_grp):
+
+        @pl.when(grp != k)
+        def _():
+            hand(k).wait_send()
 
 
 def trig_table():
@@ -405,7 +414,8 @@
             pltpu.VMEM((2,) + block, jnp.float32),
             pltpu.SemaphoreType.DMA((9,)),
             pltpu.SemaphoreType.DMA((LOADS,)),
-            pltpu.SemaphoreType.DMA((n_grp, n_grp)),
+            pltpu.SemaphoreType.REGULAR((n_grp,)),
+            pltpu.SemaphoreType.DMA((n_grp,)),
             pltpu.SemaphoreType.DMA((n_grp,)),
             pltpu.SemaphoreType.DMA((2, 2, len(CUTS[0]) - 1)),
             pltpu.SemaphoreType.DMA((2, 2, len(CUTS[0]) - 1)),

time: 23.1 us -> 22.7 us (0.983)
  Pallas kernels: 22.2 us -> 21.7 us
    pallas_call x1, Pallas kernels: 22.2 us -> 21.7 us  [shards(): pl.pallas_call(functools.partial(kernel, n_pts, n_grp), out_shape=jax.Sha...]
where the time goes in v3:
time: 22.7 us; the launch traced here: 22.6 us
  Pallas kernels  21.7 us (96%)
  local copies, waits for them, and re-layouts  0.82 us (4%)
    pallas_call x1, Pallas kernels, shards(): pl.pallas_call(functools.partial(kernel, n_pts, n_grp), out_shape=jax.Sha...  21.7 us
    unnamed x1, local copies, waits for them, and re-layouts  0.82 us

profile of v3, /device:TPU:30, one launch (start us, length us, event | category | flops | bytes accessed | tf_op | source)
XLA Modules:
  0.0 22.6 jit_solution(9937809784042346829)
XLA Ops:
  0.0 21.7 %wave_step.1 = f32[1152,128]{1,0:T(8,128)S(1)} custom-call(f32[4,36]{1,0:T(4,128)} %constant.2.clone.trig_ref, f32[1152,128]{1,0:T(8,128)} %bitcast.7, f32[16,1152]{1,0:T(8,128)} %bitcast.9, f32[1,128]{1,0:T(1,128)} %east_hbm.1, f32[1,128]{1,0:T(1,128)} %north_hbm.1, f32[1,128]{1,0:T(1,128)} %turn_hbm.1, f32[32,32]{1,0:T(8,128)} %kern_hbm.1, ...), custom_call_target="tpu_custom_call" | custom-call | tf_op jit(solution)/shard_map/wave_step/pallas_call | solution.py:396
  21.7 0.8 %copy.12 = f32[1,1152,128]{2,1,0:T(8,128)} copy(f32[1,1152,128]{2,1,0:T(8,128)S(1)} %bitcast.6) | data formatting | bytes 1179648

commit v4 on v3

--- a/solution.py
+++ b/solution.py
@@ -15,7 +15,8 @@
 QUAD = NDIR // 4
 PIECE = 3
 CUTS = ((0, 3, 9, 18, 27, 36), (0, 9, 18, 27, 33, 36))
-LOADS = 4
+EARLY = ()
+LOADS = 2
 EAGER = 2
 MESH = pl.DeviceIdType.MESH
 
@@ -200,14 +201,16 @@
         def _():
             halo(step, c, 1).wait_recv()
 
-    def sent_both(step, c):
+    def drain(copies):
         @pl.when(has_after)
         def _():
-            halo(step, c, 0).wait_send()
+            for step, c in copies:
+                halo(step, c, 0).wait_send()
 
         @pl.when(has_before)
         def _():
-            halo(step, c, 1).wait_send()
+            for step, c in copies:
+                halo(step, c, 1).wait_send()
 
     def source(first):
         cells = [spec_v[pl.ds(first + i, NFREQ, stride=NDIR), :] for i in range(PIECE)]
@@ -227,8 +230,8 @@
             mix = mixed[:, i * BLOCK : (i + 1) * BLOCK]
             own[0, d] = maskf * (cell + cell * (grow - diss) + 0.2 * mix)
 
-    parts = len(CUTS[0]) - 1
-    for c in range(parts):
+    parts = [len(cuts) - 1 for cuts in CUTS]
+    for c in range(parts[0]):
         for first in range(CUTS[0][c], CUTS[0][c + 1], PIECE):
             source(first)
         if c == 0:
@@ -267,6 +270,8 @@
     for r in range(4):
         pick_v[r] = jnp.where(window == place[r : r + 1], 1.0, 0.0).astype(jnp.bfloat16)
 
+    coarse_n[...] = jnp.zeros((comps, BLOCK), jnp.float32)
+
     def clear(into):
         def clear_one(d, carry):
             for step in range(2):
@@ -290,10 +295,9 @@
             arrival(k).wait_recv()
 
     stacked = coarse_v[...].reshape(n_grp * slots, comps)
-    pad = jnp.zeros((BLOCK - n_grp * slots, BLOCK), jnp.float32)
     for t in range(comps // BLOCK):
-        tile = jnp.concatenate([stacked[:, t * BLOCK : (t + 1) * BLOCK], pad], axis=0)
-        coarse_n[t * BLOCK : (t + 1) * BLOCK, :] = jnp.transpose(tile)
+        tile = stacked[:, t * BLOCK : (t + 1) * BLOCK]
+        coarse_n[t * BLOCK : (t + 1) * BLOCK, : n_grp * slots] = jnp.transpose(tile)
 
     def advect(step, first, end):
         quad = first // QUAD
@@ -331,12 +335,13 @@
             )
 
     got = sent = 0
-    for first in range(0, NDIR, QUAD):
-        while got < parts and CUTS[0][got] < first + QUAD:
+    edges = sorted({*range(0, NDIR + 1, QUAD), *EARLY})
+    for first, end in zip(edges, edges[1:]):
+        while got < parts[0] and CUTS[0][got] < end:
             await_both(0, got)
             got += 1
-        advect(0, first, first + QUAD)
-        while sent < parts and CUTS[1][sent + 1] <= first + QUAD:
+        advect(0, first, end)
+        while sent < parts[1] and CUTS[1][sent + 1] <= end:
             send_both(1, sent)
             sent += 1
 
@@ -350,7 +355,15 @@
         out_ref[pl.ds(d, NFREQ, stride=NDIR), :] = maskf * (mine - slow * (mine - up))
 
     done = 1
-    for c in range(parts):
+    for c in range(parts[1]):
+        if c == parts[1] - 1:
+            drain([(0, k) for k in range(parts[0])] + [(1, k) for k in range(c)])
+            for k in range(n_grp):
+
+                @pl.when(grp != k)
+                def _():
+                    hand(k).wait_send()
+
         await_both(1, c)
         advect(1, CUTS[1][c], CUTS[1][c + 1])
         while done < CUTS[1][c + 1] - 1:
@@ -359,14 +372,7 @@
     refract(NDIR - 1)
     refract(0)
 
-    for step in range(2):
-        for c in range(parts):
-            sent_both(step, c)
-    for k in range(n_grp):
-
-        @pl.when(grp != k)
-        def _():
-            hand(k).wait_send()
+    drain([(1, parts[1] - 1)])
 
 
 def trig_table():
@@ -417,8 +423,8 @@
             pltpu.SemaphoreType.REGULAR((n_grp,)),
             pltpu.SemaphoreType.DMA((n_grp,)),
             pltpu.SemaphoreType.DMA((n_grp,)),
-            pltpu.SemaphoreType.DMA((2, 2, len(CUTS[0]) - 1)),
-            pltpu.SemaphoreType.DMA((2, 2, len(CUTS[0]) - 1)),
+            pltpu.SemaphoreType.DMA((2, 2, max(map(len, CUTS)) - 1)),
+            pltpu.SemaphoreType.DMA((2, 2, max(map(len, CUTS)) - 1)),
         ],
         compiler_params=pltpu.CompilerParams(
             collective_id=0, has_side_effects=True, vmem_limit_bytes=24 * 1024 * 1024

time: 22.7 us -> 22.6 us (level)
  no operation moved by 1% of the time
where the time goes in v4:
time: 22.6 us; the launch traced here: 22.5 us
  Pallas kernels  21.6 us (96%)
  local copies, waits for them, and re-layouts  0.82 us (4%)
    pallas_call x1, Pallas kernels, shards(): pl.pallas_call(functools.partial(kernel, n_pts, n_grp), out_shape=jax.Sha...  21.6 us
    unnamed x1, local copies, waits for them, and re-layouts  0.82 us

profile of v4, /device:TPU:30, one launch (start us, length us, event | category | flops | bytes accessed | tf_op | source)
XLA Modules:
  0.0 22.5 jit_solution(1432141321461557202)
XLA Ops:
  0.0 21.6 %wave_step.1 = f32[1152,128]{1,0:T(8,128)S(1)} custom-call(f32[4,36]{1,0:T(4,128)} %constant.2.clone.trig_ref, f32[1152,128]{1,0:T(8,128)} %bitcast.7, f32[16,1152]{1,0:T(8,128)} %bitcast.9, f32[1,128]{1,0:T(1,128)} %east_hbm.1, f32[1,128]{1,0:T(1,128)} %north_hbm.1, f32[1,128]{1,0:T(1,128)} %turn_hbm.1, f32[32,32]{1,0:T(8,128)} %kern_hbm.1, ...), custom_call_target="tpu_custom_call" | custom-call | tf_op jit(solution)/shard_map/wave_step/pallas_call | solution.py:402
  21.7 0.8 %copy.12 = f32[1,1152,128]{2,1,0:T(8,128)} copy(f32[1,1152,128]{2,1,0:T(8,128)S(1)} %bitcast.6) | data formatting | bytes 1179648

commit v5 on v4

--- a/solution.py
+++ b/solution.py
@@ -299,30 +299,42 @@
         tile = stacked[:, t * BLOCK : (t + 1) * BLOCK]
         coarse_n[t * BLOCK : (t + 1) * BLOCK, : n_grp * slots] = jnp.transpose(tile)
 
-    def advect(step, first, end):
+    def look_up(step, first, end, places):
         quad = first // QUAD
+        lists = [(quad + 1) // 2 % 2, 2 + quad // 2]
+        cells = (end - first) * NFREQ
         picks = jnp.concatenate(
-            [pick_v[(quad + 1) // 2 % 2], pick_v[2 + quad // 2]], axis=1
-        )
-        cells = (end - first) * NFREQ
-        windows = jnp.concatenate(
             [
-                prv[step, first:end].reshape(cells, BLOCK),
-                own[step, first:end].reshape(cells, BLOCK),
-                nxt[step, first:end].reshape(cells, BLOCK),
                 jnp.concatenate(
+                    [pick_v[r, p * BLOCK : (p + 1) * BLOCK] for p in places], axis=0
+                )
+                for r in lists
+            ],
+            axis=1,
+        )
+        sources = []
+        for p in places:
+            if p < 3:
+                block = (prv, own, nxt)[p][step, first:end].reshape(cells, BLOCK)
+            else:
+                block = jnp.concatenate(
                     [coarse_n[pl.ds(d, NFREQ, stride=NDIR), :] for d in range(first, end)],
                     axis=0,
-                ),
-            ],
-            axis=1,
-        )
+                )
+            sources.append(block)
+        windows = jnp.concatenate(sources, axis=1)
         high = windows.astype(jnp.bfloat16)
         low = (windows - high.astype(jnp.float32)).astype(jnp.bfloat16)
         both = jnp.dot(
             jnp.concatenate([high, low], axis=0), picks, preferred_element_type=jnp.float32
         )
-        found = both[:cells] + both[cells:]
+        return both[:cells] + both[cells:]
+
+    def advect(step, first, end, at_hand=None):
+        if at_hand is None:
+            found = look_up(step, first, end, (0, 1, 2, 3))
+        else:
+            found = at_hand + look_up(step, first, end, (0, 2))
         for d in range(first, end):
             cell = own[step, d]
             at = (d - first) * NFREQ
@@ -356,7 +368,9 @@
 
     done = 1
     for c in range(parts[1]):
+        at_hand = None
         if c == parts[1] - 1:
+            at_hand = look_up(1, CUTS[1][c], CUTS[1][c + 1], (1, 3))
             drain([(0, k) for k in range(parts[0])] + [(1, k) for k in range(c)])
             for k in range(n_grp):
 
@@ -365,7 +379,7 @@
                     hand(k).wait_send()
 
         await_both(1, c)
-        advect(1, CUTS[1][c], CUTS[1][c + 1])
+        advect(1, CUTS[1][c], CUTS[1][c + 1], at_hand)
         while done < CUTS[1][c + 1] - 1:
             refract(done)
             done += 1

time: 22.6 us -> 22.5 us (level)
  no operation moved by 1% of the time
where the time goes in v5:
time: 22.5 us; the launch traced here: 22.4 us
  Pallas kernels  21.6 us (96%)
  local copies, waits for them, and re-layouts  0.82 us (4%)
    pallas_call x1, Pallas kernels, shards(): pl.pallas_call(functools.partial(kernel, n_pts, n_grp), out_shape=jax.Sha...  21.6 us
    unnamed x1, local copies, waits for them, and re-layouts  0.82 us

profile of v5, /device:TPU:30, one launch (start us, length us, event | category | flops | bytes accessed | tf_op | source)
XLA Modules:
  0.0 22.4 jit_solution(4495046861666722061)
XLA Ops:
  0.0 21.6 %wave_step.1 = f32[1152,128]{1,0:T(8,128)S(1)} custom-call(f32[4,36]{1,0:T(4,128)} %constant.2.clone.trig_ref, f32[1152,128]{1,0:T(8,128)} %bitcast.7, f32[16,1152]{1,0:T(8,128)} %bitcast.9, f32[1,128]{1,0:T(1,128)} %east_hbm.1, f32[1,128]{1,0:T(1,128)} %north_hbm.1, f32[1,128]{1,0:T(1,128)} %turn_hbm.1, f32[32,32]{1,0:T(8,128)} %kern_hbm.1, ...), custom_call_target="tpu_custom_call" | custom-call | tf_op jit(solution)/shard_map/wave_step/pallas_call | solution.py:416
  21.6 0.8 %copy.12 = f32[1,1152,128]{2,1,0:T(8,128)} copy(f32[1,1152,128]{2,1,0:T(8,128)S(1)} %bitcast.6) | data formatting | bytes 1179648

commit v6 on v5

--- a/solution.py
+++ b/solution.py
@@ -288,17 +288,6 @@
     def _():
         clear(nxt)
 
-    for k in range(n_grp):
-
-        @pl.when(grp != k)
-        def _():
-            arrival(k).wait_recv()
-
-    stacked = coarse_v[...].reshape(n_grp * slots, comps)
-    for t in range(comps // BLOCK):
-        tile = stacked[:, t * BLOCK : (t + 1) * BLOCK]
-        coarse_n[t * BLOCK : (t + 1) * BLOCK, : n_grp * slots] = jnp.transpose(tile)
-
     def look_up(step, first, end, places):
         quad = first // QUAD
         lists = [(quad + 1) // 2 % 2, 2 + quad // 2]
@@ -330,11 +319,28 @@
         )
         return both[:cells] + both[cells:]
 
-    def advect(step, first, end, at_hand=None):
+    got = 0
+    while got < parts[0] and CUTS[0][got] < QUAD:
+        await_both(0, got)
+        got += 1
+    nearby = look_up(0, 0, QUAD, (0, 1, 2))
+
+    for k in range(n_grp):
+
+        @pl.when(grp != k)
+        def _():
+            arrival(k).wait_recv()
+
+    stacked = coarse_v[...].reshape(n_grp * slots, comps)
+    for t in range(comps // BLOCK):
+        tile = stacked[:, t * BLOCK : (t + 1) * BLOCK]
+        coarse_n[t * BLOCK : (t + 1) * BLOCK, : n_grp * slots] = jnp.transpose(tile)
+
+    def advect(step, first, end, at_hand=None, left=(0, 2)):
         if at_hand is None:
             found = look_up(step, first, end, (0, 1, 2, 3))
         else:
-            found = at_hand + look_up(step, first, end, (0, 2))
+            found = at_hand + look_up(step, first, end, left)
         for d in range(first, end):
             cell = own[step, d]
             at = (d - first) * NFREQ
@@ -346,13 +352,13 @@
                 cell - step_x * (cell - from_x) - step_y * (cell - from_y)
             )
 
-    got = sent = 0
+    sent = 0
     edges = sorted({*range(0, NDIR + 1, QUAD), *EARLY})
     for first, end in zip(edges, edges[1:]):
         while got < parts[0] and CUTS[0][got] < end:
             await_both(0, got)
             got += 1
-        advect(0, first, end)
+        advect(0, first, end, None if first else nearby, (3,))
         while sent < parts[1] and CUTS[1][sent + 1] <= end:
             send_both(1, sent)
             sent += 1

time: 22.5 us -> 22.9 us (1.018)
  Pallas kernels: 21.6 us -> 22 us
    pallas_call x1, Pallas kernels: 21.6 us -> 22 us  [shards(): pl.pallas_call(functools.partial(kernel, n_pts, n_grp), out_shape=jax.Sha...]
where the time goes in v6:
time: 22.9 us; the launch traced here: 22.8 us
  Pallas kernels  22 us (96%)
  local copies, waits for them, and re-layouts  0.82 us (4%)
    pallas_call x1, Pallas kernels, shards(): pl.pallas_call(functools.partial(kernel, n_pts, n_grp), out_shape=jax.Sha...  22 us
    unnamed x1, local copies, waits for them, and re-layouts  0.82 us

profile of v6, /device:TPU:30, one launch (start us, length us, event | category | flops | bytes accessed | tf_op | source)
XLA Modules:
  0.0 22.8 jit_solution(8401109074006947864)
XLA Ops:
  0.0 22.0 %wave_step.1 = f32[1152,128]{1,0:T(8,128)S(1)} custom-call(f32[4,36]{1,0:T(4,128)} %constant.2.clone.trig_ref, f32[1152,128]{1,0:T(8,128)} %bitcast.7, f32[16,1152]{1,0:T(8,128)} %bitcast.9, f32[1,128]{1,0:T(1,128)} %east_hbm.1, f32[1,128]{1,0:T(1,128)} %north_hbm.1, f32[1,128]{1,0:T(1,128)} %turn_hbm.1, f32[32,32]{1,0:T(8,128)} %kern_hbm.1, ...), custom_call_target="tpu_custom_call" | custom-call | tf_op jit(solution)/shard_map/wave_step/pallas_call | solution.py:422
  22.0 0.8 %copy.12 = f32[1,1152,128]{2,1,0:T(8,128)} copy(f32[1,1152,128]{2,1,0:T(8,128)S(1)} %bitcast.6) | data formatting | bytes 1179648
